TPU v7x, 32 devices: a whole 2x2x4 slice. The times are simulated.
32 devices in a mesh: head: 2 (over core), ctx: 16 (over z, y, x).
Axes of the slice: x: 2, y: 2, z: 4, core: 2. Of those that a mesh axis runs over, the one named last changes fastest.
Arguments:
- queries: bfloat16 [4096, 4096], P(('ctx', 'head')), may hold values from -6 to 6
- keys: bfloat16 [4096, 512], P(('ctx', 'head')), may hold values from -6 to 6
- values: bfloat16 [4096, 512], P(('ctx', 'head')), may hold values from -6 to 6
- attn_out: bfloat16 [4096, 4096], P(('ctx', 'head')), may hold values from -6 to 6
- output_gradient: bfloat16 [4096, 4096], P(('ctx', 'head')), may hold values from -6 to 6
- doc_lengths: int32 [32], replicated, may hold values from 1 to 257, 4096 in all
Outputs:
- query_grad: bfloat16 [4096, 4096], P(('ctx', 'head'))
- key_gradient: bfloat16 [4096, 512], P(('ctx', 'head'))
- value_gradient: bfloat16 [4096, 512], P(('ctx', 'head'))
Inputs may be any that keep to these rules, and one draw needn't show every extreme that they name: `doc_lengths`: documents fill the 4096 tokens in order; one document has exactly 257 tokens.
All inputs are finite; a program needn't handle non-finite values.
Results may differ from a plain program's by a relative error of at most 0.0054.
Values may be sent and summed in bfloat16 or wider, within the bound.
A program may use at most 64 MiB of HBM per device.

v0:
```python
import jax
import jax.numpy as jnp
from jax import lax
from jax.sharding import PartitionSpec as P

QUERY_HEAD_COUNT = 32
KEY_VALUE_HEADS = 4
HEAD_SIZE = 128
REACH = 1


fill_value = -1e30


def shifted(shard, axis, by):
    size = lax.axis_size(axis)
    pairs = [(i, i + by) for i in range(size) if 0 <= i + by < size]
    return lax.ppermute(shard, axis, pairs)


def segment_ids(doc_lengths, positions):
    ends = jnp.cumsum(doc_lengths)
    found = jnp.sum(
        (ends[None, :] <= positions[:, None]).astype(jnp.int32), axis=1, dtype=jnp.int32
    )
    return jnp.where(positions >= 0, found, -1)


def kv_window(key_part, value_part):
    window = [(key_part, value_part)]
    window.append(shifted((key_part, value_part), "ctx", 1))
    return window


def grad_return(key_parts, value_parts):
    key_total = key_parts[0]
    value_total = value_parts[0]
    back_key, back_value = shifted((key_parts[1], value_parts[1]), "ctx", -1)
    key_total = key_total + back_key
    value_total = value_total + back_value
    return (key_total, value_total)


def on_device(queries, keys, values, attn_out, output_gradient, doc_lengths):
    local_rows = queries.shape[0]
    group_width = QUERY_HEAD_COUNT // KEY_VALUE_HEADS
    score_scale = HEAD_SIZE ** (-0.5)
    delta_value = jnp.sum(
        (output_gradient.astype(jnp.float32) * attn_out.astype(jnp.float32)).reshape(
            local_rows, QUERY_HEAD_COUNT, HEAD_SIZE
        ),
        axis=2,
    ).astype(jnp.bfloat16)
    shard_index = lax.axis_index("ctx")
    query_side, grad_side, delta_side, key_side, value_side = (
        lax.all_to_all(queries, "head", split_axis=1, concat_axis=0, tiled=True),
        lax.all_to_all(output_gradient, "head", split_axis=1, concat_axis=0, tiled=True),
        lax.all_to_all(delta_value, "head", split_axis=1, concat_axis=0, tiled=True),
        lax.all_to_all(keys, "head", split_axis=1, concat_axis=0, tiled=True),
        lax.all_to_all(values, "head", split_axis=1, concat_axis=0, tiled=True),
    )
    first_row = shard_index * query_side.shape[0]
    window = kv_window(key_side, value_side)
    query_row_block = query_side.shape[0]
    key_rows = window[0][0].shape[0]
    kv_local = window[0][0].shape[1] // HEAD_SIZE
    query_heads = query_side.reshape(query_row_block, kv_local, group_width, HEAD_SIZE)
    grad_heads = grad_side.reshape(query_row_block, kv_local, group_width, HEAD_SIZE)
    row_delta_values = jnp.transpose(
        delta_side.reshape(query_row_block, kv_local, group_width).astype(jnp.float32), (1, 2, 0)
    )
    pos_query = first_row + jnp.arange(query_row_block, dtype=jnp.int32)
    seg_query = segment_ids(doc_lengths, pos_query)
    key_index = jnp.arange(key_rows, dtype=jnp.int32)
    bias_list = []
    live_list = []
    for offset in range(REACH + 1):
        pos_key = (shard_index - offset) * key_rows + key_index
        seg_key = segment_ids(doc_lengths, pos_key)
        allowed = (seg_query[:, None] == seg_key[None, :]) & (
            pos_key[None, :] <= pos_query[:, None]
        )
        bias_list.append(jnp.where(allowed, 0.0, fill_value).astype(jnp.float32))
        live_list.append(jnp.logical_and(seg_key[-1] == seg_query[0], seg_key[-1] >= 0))

    def tile_scores(key_tile, bias):
        key_heads = key_tile.reshape(key_rows, kv_local, HEAD_SIZE)
        return (
            jnp.einsum("tkgd,ukd->kgtu", query_heads, key_heads, preferred_element_type=jnp.float32)
            * score_scale
            + bias
        )

    stat_shape = (kv_local, group_width, query_row_block)
    row_max = jnp.full(stat_shape, fill_value, jnp.float32)
    row_sum = jnp.zeros(stat_shape, jnp.float32)
    for offset in range(REACH + 1):
        key_tile = window[offset][0]
        bias = bias_list[offset]
        masked = tile_scores(key_tile, bias)
        tile_max = jnp.max(masked, axis=-1)
        tile_sum = jnp.sum(jnp.exp(masked - tile_max[..., None]), axis=-1)
        tile_sum = jnp.where(tile_max > 0.5 * fill_value, tile_sum, 0.0)
        tile_max, tile_sum = (tile_max, tile_sum)
        new_max = jnp.maximum(row_max, tile_max)
        row_sum = row_sum * jnp.exp(row_max - new_max) + tile_sum * jnp.exp(tile_max - new_max)
        row_max = new_max
    lse = row_max + jnp.log(row_sum)
    query_total = jnp.zeros((query_row_block, kv_local, group_width, HEAD_SIZE), jnp.float32)
    key_parts = []
    value_parts = []
    for offset in range(REACH + 1):
        key_tile, value_tile = window[offset]
        bias = bias_list[offset]
        tile_key_heads = key_tile.reshape(key_rows, kv_local, HEAD_SIZE)
        value_heads = value_tile.reshape(key_rows, kv_local, HEAD_SIZE)
        probs = jnp.exp(tile_scores(key_tile, bias) - lse[..., None])
        probs_low = probs.astype(jnp.bfloat16)
        prob_grad = jnp.einsum(
            "tkgd,ukd->kgtu", grad_heads, value_heads, preferred_element_type=jnp.float32
        )
        score_grad = (probs * (prob_grad - row_delta_values[..., None])).astype(jnp.bfloat16)
        query_part = (
            jnp.einsum(
                "kgtu,ukd->tkgd", score_grad, tile_key_heads, preferred_element_type=jnp.float32
            )
            * score_scale
        )
        key_part = (
            jnp.einsum(
                "kgtu,tkgd->ukd", score_grad, query_heads, preferred_element_type=jnp.float32
            )
            * score_scale
        )
        value_part = jnp.einsum(
            "kgtu,tkgd->ukd", probs_low, grad_heads, preferred_element_type=jnp.float32
        )
        query_part, key_part, value_part = (
            query_part,
            key_part.reshape(key_rows, kv_local * HEAD_SIZE),
            value_part.reshape(key_rows, kv_local * HEAD_SIZE),
        )
        query_total = query_total + query_part
        key_parts.append(key_part)
        value_parts.append(value_part)
    query_low = query_total.reshape(query_row_block, kv_local * group_width * HEAD_SIZE).astype(
        jnp.bfloat16
    )
    key_total, value_total = grad_return(key_parts, value_parts)
    query_grad, key_gradient, value_gradient = (
        lax.all_to_all(query_low, "head", split_axis=0, concat_axis=1, tiled=True),
        lax.all_to_all(
            key_total.astype(jnp.bfloat16), "head", split_axis=0, concat_axis=1, tiled=True
        ),
        lax.all_to_all(
            value_total.astype(jnp.bfloat16), "head", split_axis=0, concat_axis=1, tiled=True
        ),
    )
    return (query_grad, key_gradient, value_gradient)


def solution(mesh):
    in_specs = (
        P(("ctx", "head"), None),
        P(("ctx", "head"), None),
        P(("ctx", "head"), None),
        P(("ctx", "head"), None),
        P(("ctx", "head"), None),
        P(),
    )
    out_specs = (P(("ctx", "head"), None), P(("ctx", "head"), None), P(("ctx", "head"), None))
    return jax.shard_map(
        on_device, mesh=mesh, in_specs=in_specs, out_specs=out_specs, check_vma=False
    )
```

profile of v0, /device:TPU:17, one launch (start us, length us, event | category | flops | bytes accessed | tf_op | source)
XLA Modules:
  0.0 92.3 jit_solution(15344815339688610074)
XLA Ops:
  0.7 1.8 %copy.219 = bf16[128,512]{0,1:T(8,128)(2,1)} copy(bf16[128,512]{1,0:T(8,128)(2,1)} %param.8) | data formatting | bytes 262144 | tf_op args[2]
  2.4 4.0 %all-to-all-start.2 = ((bf16[128,2,256]{0,2,1:T(8,128)(2,1)}), bf16[128,2,256]{0,2,1:T(8,128)(2,1)S(1)}, u32[]{:S(2)}, u32[]{:S(2)}) async-start(bf16[128,2,256]{0,2,1:T(8,128)(2,1)} %bitcast.10), calls=%async_computation.2 | async-start | bytes 262144 | tf_op jit(solution)/shard_map/all_to_all | solution.py:60
  6.4 1.7 %copy.209 = bf16[128,512]{0,1:T(8,128)(2,1)} copy(bf16[128,512]{1,0:T(8,128)(2,1)} %param.7) | data formatting | bytes 262144 | tf_op args[1]
  8.1 3.4 %all-to-all-start = ((bf16[128,2,256]{0,2,1:T(8,128)(2,1)}), bf16[128,2,256]{0,2,1:T(8,128)(2,1)S(1)}, u32[]{:S(2)}, u32[]{:S(2)}) async-start(bf16[128,2,256]{0,2,1:T(8,128)(2,1)} %bitcast), calls=%async_computation | async-start | bytes 262144 | tf_op jit(solution)/shard_map/all_to_all | solution.py:59
  11.6 3.1 %collective-permute-start.1 = (bf16[256,256]{1,0:T(8,128)(2,1)S(1)}, bf16[256,256]{1,0:T(8,128)(2,1)}, u32[]{:S(2)}, u32[]{:S(2)}) collective-permute-start(bf16[256,256]{1,0:T(8,128)(2,1)S(1)} %bitcast.159), channel_id=1, source_target_pairs={{0,1},{1,2},{2,3},{3,4},{4,5},{5,6},{6,7},{7,8},{8,9},{9,10},{10,1... | collective-permute-start | bytes 393224 | tf_op jit(solution)/shard_map/ppermute | solution.py:18
  14.8 0.8 copy.210
  15.5 3.1 %collective-permute-start = (bf16[256,256]{1,0:T(8,128)(2,1)}, bf16[256,256]{1,0:T(8,128)(2,1)}, u32[]{:S(2)}, u32[]{:S(2)}) collective-permute-start(bf16[256,256]{1,0:T(8,128)(2,1)} %bitcast.6), channel_id=1, source_target_pairs={{0,1},{1,2},{2,3},{3,4},{4,5},{5,6},{6,7},{7,8},{8,9},{9,10},{10,1... | collective-permute-start | bytes 393224 | tf_op jit(solution)/shard_map/ppermute | solution.py:18
  18.7 2.3 %copy.295 = bf16[16,2,8,2048]{3,2,0,1:T(8,128)(2,1)} copy(bf16[16,2,8,2048]{3,2,1,0:T(8,128)(2,1)} %bitcast.156) | data formatting | bytes 2097152 | tf_op jit(solution)/shard_map/all_to_all | solution.py:56
  21.0 4.2 %all-to-all-start.1 = ((bf16[128,2,2048]{2,0,1:T(8,128)(2,1)}), bf16[128,2,2048]{2,0,1:T(8,128)(2,1)S(1)}, u32[]{:S(2)}, u32[]{:S(2)}) async-start(bf16[128,2,2048]{2,0,1:T(8,128)(2,1)} %bitcast.144), calls=%async_computation.1 | async-start | bytes 2097152 | tf_op jit(solution)/shard_map/all_to_all | solution.py:56
  25.1 0.9 %reshape.283 = bf16[256,2,128]{2,1,0:T(2,128)(2,1)S(1)} reshape(bf16[2,128,256]{2,1,0:T(8,128)(2,1)} %copy.210) | data formatting | bytes 262144 | tf_op jit(solution)/shard_map/reshape | solution.py:115
  26.3 0.7 reduce
  27.0 1.1 %copy.294 = bf16[16,2,8,2048]{3,2,0,1:T(8,128)(2,1)} copy(bf16[16,2,8,2048]{3,2,1,0:T(8,128)(2,1)S(1)} %bitcast.151) | data formatting | bytes 2097152 | tf_op jit(solution)/shard_map/all_to_all | solution.py:57
  28.1 4.4 %all-to-all-start.3 = ((bf16[128,2,2048]{2,0,1:T(8,128)(2,1)}), bf16[128,2,2048]{2,0,1:T(8,128)(2,1)}, u32[]{:S(2)}, u32[]{:S(2)}) async-start(bf16[128,2,2048]{2,0,1:T(8,128)(2,1)} %bitcast.143), calls=%async_computation.3 | async-start | bytes 2097152 | tf_op jit(solution)/shard_map/all_to_all | solution.py:57
  32.7 0.8 copy.237
  33.5 1.5 %multiply_bitcast_fusion = f32[16,8,32,128]{3,1,2,0:T(8,128)S(1)} fusion(bf16[128,4096]{1,0:T(8,128)(2,1)} %param.9, bf16[128,4096]{1,0:T(8,128)(2,1)S(1)} %copy-done.6), kind=kLoop, calls=%fused_computation.17 | loop fusion | flops 1572864 | bytes 4194304
  35.3 1.2 %reduce_sum.53 = bf16[128,32]{1,0:T(8,128)(2,1)} reduce(f32[128,32,128]{2,1,0:T(8,128)S(1)} %bitcast.145, f32[]{:T(128)} %constant.14.clone.1), dimensions={2}, to_apply=%region_7.8 | reduce | flops 520192 | bytes 2105348 | tf_op jit(solution)/shard_map/reduce_sum | solution.py:48
  36.6 1.4 %copy.224 = bf16[128,32]{0,1:T(8,128)(2,1)} copy(bf16[128,32]{1,0:T(8,128)(2,1)} %reduce_sum.53) | data formatting | bytes 16384 | tf_op jit(solution)/shard_map/reduce_sum | solution.py:48
  38.0 3.4 %all-to-all-start.4 = ((bf16[128,2,16]{0,2,1:T(8,128)(2,1)}), bf16[128,2,16]{0,2,1:T(8,128)(2,1)S(1)}, u32[]{:S(2)}, u32[]{:S(2)}) async-start(bf16[128,2,16]{0,2,1:T(8,128)(2,1)} %bitcast.15), calls=%async_computation.4 | async-start | bytes 16384 | tf_op jit(solution)/shard_map/all_to_all | solution.py:58
  41.4 1.4 %copy.282 = bf16[32,8,16,128]{3,2,1,0:T(8,128)(2,1)S(1)} copy(bf16[32,8,16,128]{3,1,2,0:T(8,128)(2,1)} %bitcast.72) | data formatting | bytes 2097152
  42.9 0.8 copy.243
  43.7 0.7 convert_reduce_fusion
  44.7 0.7 fusion.6
  45.4 2.0 %copy-done = f32[2,256,256,8]{2,1,3,0:T(8,128)} copy-done((f32[2,256,256,8]{2,1,3,0:T(8,128)}, f32[2,256,256,8]{2,1,3,0:T(8,128)S(1)}, u32[]{:S(2)}) %copy-start) | copy-done | bytes 4194328
  47.3 0.8 exponential_reduce_fusion.1
  48.3 1.0 %copy.216 = bf16[256,256]{0,1:T(8,128)(2,1)S(1)} copy(bf16[256,256]{1,0:T(8,128)(2,1)} %collective-permute-done) | data formatting | bytes 262144 | tf_op jit(solution)/shard_map/ppermute | solution.py:18
  49.3 0.8 fusion.7
  50.1 0.8 exponential_reduce_fusion
  50.9 1.7 %copy-done.1 = f32[2,256,256,8]{2,1,3,0:T(8,128)S(1)} copy-done((f32[2,256,256,8]{2,1,3,0:T(8,128)S(1)}, f32[2,256,256,8]{2,1,3,0:T(8,128)}, u32[]{:S(2)}) %copy-start.1) | copy-done | bytes 4194328
  52.6 1.1 %fusion.10 = f32[2,256,128,1]{1,2,3,0:T(8,128)S(1)} fusion(bf16[256,2,8,128]{0,3,2,1:T(8,128)(2,1)S(1)} %copy.243, f32[2,256,256,8]{2,1,3,0:T(8,128)S(1)} %copy-done.1, f32[2,8,256]{2,1,0:T(8,128)S(1)} %fusion.28, f32[256,256]{0,1:T(8,128)S(1)} %get-tuple-element.21), kind=kOutput, calls=%fused_computation.19 | convolution fusion | flops 272629760 | bytes 5783552 | tf_op jit(solution)/shard_map/kgtu,tkgd->ukd/dot_general | solution.py:135
  53.8 1.8 %fusion.8 = f32[2,256,128,1]{1,2,3,0:T(8,128)} fusion(bf16[256,2,8,128]{0,3,2,1:T(8,128)(2,1)S(1)} %copy.243, f32[2,256,256,8]{2,1,3,0:T(8,128)S(1)} %get-tuple-element.25, f32[2,8,256]{2,1,0:T(8,128)S(1)} %fusion.28, f32[256,256]{0,1:T(8,128)S(1)} %get-tuple-element.20), kind=kOutput, calls=%fused_computation.18 | convolution fusion | flops 272629760 | bytes 5783552 | tf_op jit(solution)/shard_map/kgtu,tkgd->ukd/dot_general | solution.py:135
  55.6 1.2 %fusion.3 = bf16[2,8,256,256]{2,3,1,0:T(8,128)(2,1)S(1)} fusion(f32[2,256,256,8]{2,1,3,0:T(8,128)S(1)} %copy-done.1, bf16[256,2,8,128]{0,3,2,1:T(8,128)(2,1)S(1)} %copy.243, f32[2,8,256]{2,1,0:T(8,128)S(1)} %bitcast.167, f32[2,8,256]{2,1,0:T(8,128)S(1)} %fusion.28, f32[256,256]{0,1:T(8,128)S(1)} %get-tuple-element.21, bf16[256,2,128,1]{2,1,0,3:T(2,128)(2,1)S(1)} %bitcast.157), kind=kOutput, calls=%fused_computation.5 | convolution fusion | flops 274726912 | bytes 7766016 | tf_op jit(solution)/shard_map/tkgd,ukd->kgtu/dot_general | solution.py:119
  56.8 1.3 %copy-done.3 = bf16[2,8,256,256]{2,3,1,0:T(8,128)(2,1)} copy-done((bf16[2,8,256,256]{2,3,1,0:T(8,128)(2,1)}, bf16[2,8,256,256]{2,3,1,0:T(8,128)(2,1)S(1)}, u32[]{:S(2)}) %copy-start.3) | copy-done | bytes 2097176
  58.2 2.3 %fusion.18 = f32[2,8,256,128]{3,2,1,0:T(8,128)} fusion(bf16[2,8,256,256]{2,3,1,0:T(8,128)(2,1)S(1)} %fusion.3, bf16[256,2,128,1]{2,1,0,3:T(2,128)(2,1)S(1)} %bitcast.153), kind=kOutput, calls=%fused_computation.34 | convolution fusion | flops 268435456 | bytes 4325376 | tf_op jit(solution)/shard_map/kgtu,ukd->tkgd/dot_general | solution.py:124
  60.4 1.0 %copy.229 = bf16[256,256]{0,1:T(8,128)(2,1)S(1)} copy(bf16[256,256]{1,0:T(8,128)(2,1)} %collective-permute-done.1) | data formatting | bytes 262144 | tf_op jit(solution)/shard_map/ppermute | solution.py:18
  61.5 3.6 %fusion.1 = bf16[2,8,256,256]{2,3,1,0:T(8,128)(2,1)S(1)} fusion(f32[2,256,256,8]{2,1,3,0:T(8,128)} %copy-done.2, bf16[256,2,128,1]{0,2,3,1:T(8,128)(2,1)S(1)} %bitcast.158, bf16[256,2,8,128]{0,3,2,1:T(8,128)(2,1)S(1)} %copy.243, f32[2,8,256]{2,1,0:T(8,128)S(1)} %bitcast.168, f32[2,8,256]{2,1,0:T(8,128)S(1)} %fusion.28, f32[256,256]{0,1:T(8,128)S(1)} %get-tuple-element.20), kind=kOutput, calls=%fused_computation.2 | convolution fusion | flops 274726912 | bytes 7766016 | tf_op jit(solution)/shard_map/tkgd,ukd->kgtu/dot_general | solution.py:119
  65.1 1.5 %fusion.13 = f32[2,256,128]{1,2,0:T(8,128)} fusion(bf16[2,8,256,256]{2,3,1,0:T(8,128)(2,1)S(1)} %fusion.1, bf16[256,2,8,128]{0,3,2,1:T(8,128)(2,1)S(1)} %copy.237), kind=kOutput, calls=%fused_computation.22 | convolution fusion | flops 268500992 | bytes 3407872 | tf_op jit(solution)/shard_map/kgtu,tkgd->ukd/dot_general | solution.py:130
  66.6 1.0 %fusion.12 = bf16[256,2,8,128]{3,0,2,1:T(8,128)(2,1)S(1)} fusion(f32[2,8,256,128]{3,2,1,0:T(8,128)S(1)} %copy-done.5, bf16[2,8,256,256]{2,3,1,0:T(8,128)(2,1)S(1)} %fusion.1, bf16[256,2,128,1]{0,2,3,1:T(8,128)(2,1)S(1)} %bitcast.155), kind=kOutput, calls=%fused_computation.20 | convolution fusion | flops 270008320 | bytes 5373952 | tf_op jit(solution)/shard_map/kgtu,ukd->tkgd/dot_general | solution.py:124
  67.6 4.0 %collective-permute-start.3 = (f32[256,256]{0,1:T(8,128)S(1)}, f32[256,256]{0,1:T(8,128)S(1)}, u32[]{:S(2)}, u32[]{:S(2)}) collective-permute-start(f32[256,256]{0,1:T(8,128)S(1)} %bitcast.166), channel_id=1, source_target_pairs={{1,0},{2,1},{3,2},{4,3},{5,4},{6,5},{7,6},{8,7},{9,8},{10,9},{11,1... | collective-permute-start | bytes 786440 | tf_op jit(solution)/shard_map/ppermute | solution.py:18
  71.6 2.2 %collective-permute-start.2 = (f32[256,256]{0,1:T(8,128)}, f32[256,256]{0,1:T(8,128)S(1)}, u32[]{:S(2)}, u32[]{:S(2)}) collective-permute-start(f32[256,256]{0,1:T(8,128)} %bitcast.34), channel_id=1, source_target_pairs={{1,0},{2,1},{3,2},{4,3},{5,4},{6,5},{7,6},{8,7},{9,8},{10,9},{11,1... | collective-permute-start | bytes 786440 | tf_op jit(solution)/shard_map/ppermute | solution.py:18
  73.7 0.8 fusion.14
  74.5 0.7 copy.234
  75.7 4.8 %all_to_all.134 = bf16[2,128,2048]{2,1,0:T(8,128)(2,1)S(1)} all-to-all(bf16[2,128,2048]{2,1,0:T(8,128)(2,1)S(1)} %convert_element_type.67), channel_id=1, replica_groups=mesh['head'=2,'ctx'=16] {'head'}, dimensions={0} | all-to-all | bytes 2097152 | tf_op jit(solution)/shard_map/all_to_all | solution.py:151
  80.5 0.7 copy.235
  81.2 1.3 %copy.248 = bf16[128,4096]{1,0:T(8,128)(2,1)} copy(bf16[128,4096]{0,1:T(8,128)(2,1)S(1)} %bitcast.150) | data formatting | bytes 2097152
  82.6 3.9 %all_to_all.135 = bf16[2,128,256]{2,1,0:T(8,128)(2,1)S(1)} all-to-all(bf16[2,128,256]{2,1,0:T(8,128)(2,1)S(1)} %bitcast.162), channel_id=1, replica_groups=mesh['head'=2,'ctx'=16] {'head'}, dimensions={0} | all-to-all | bytes 262144 | tf_op jit(solution)/shard_map/all_to_all | solution.py:155
  86.6 0.8 copy.250
  87.5 3.8 %all_to_all.136 = bf16[2,128,256]{2,1,0:T(8,128)(2,1)S(1)} all-to-all(bf16[2,128,256]{2,1,0:T(8,128)(2,1)S(1)} %bitcast.164), channel_id=1, replica_groups=mesh['head'=2,'ctx'=16] {'head'}, dimensions={0} | all-to-all | bytes 262144 | tf_op jit(solution)/shard_map/all_to_all | solution.py:152
  91.5 0.8 copy.249
  (45 shorter events, 2.2 us)
Async XLA Ops:
  0.6 25.5 %copy-start.8 = (s32[32]{0:T(128)S(1)}, s32[32]{0:T(128)}, u32[]{:S(2)}) copy-start(s32[32]{0:T(128)} %param.11) | copy-start | bytes 388
  0.6 26.3 %copy-start.6 = (bf16[128,4096]{1,0:T(8,128)(2,1)S(1)}, bf16[128,4096]{1,0:T(8,128)(2,1)}, u32[]{:S(2)}) copy-start(bf16[128,4096]{1,0:T(8,128)(2,1)} %param.10) | copy-start | bytes 3145732
  2.4 5.7 %all-to-all-start.2 = ((bf16[128,2,256]{0,2,1:T(8,128)(2,1)}), bf16[128,2,256]{0,2,1:T(8,128)(2,1)S(1)}, u32[]{:S(2)}, u32[]{:S(2)}) async-start(bf16[128,2,256]{0,2,1:T(8,128)(2,1)} %bitcast.10), calls=%async_computation.2 | async-start | bytes 262144 | tf_op jit(solution)/shard_map/all_to_all | solution.py:60
  8.1 6.6 %all-to-all-start = ((bf16[128,2,256]{0,2,1:T(8,128)(2,1)}), bf16[128,2,256]{0,2,1:T(8,128)(2,1)S(1)}, u32[]{:S(2)}, u32[]{:S(2)}) async-start(bf16[128,2,256]{0,2,1:T(8,128)(2,1)} %bitcast), calls=%async_computation | async-start | bytes 262144 | tf_op jit(solution)/shard_map/all_to_all | solution.py:59
  11.6 48.8 %collective-permute-start.1 = (bf16[256,256]{1,0:T(8,128)(2,1)S(1)}, bf16[256,256]{1,0:T(8,128)(2,1)}, u32[]{:S(2)}, u32[]{:S(2)}) collective-permute-start(bf16[256,256]{1,0:T(8,128)(2,1)S(1)} %bitcast.159), channel_id=1, source_target_pairs={{0,1},{1,2},{2,3},{3,4},{4,5},{5,6},{6,7},{7,8},{8,9},{9,10},{10,1... | collective-permute-start | bytes 393224 | tf_op jit(solution)/shard_map/ppermute | solution.py:18
  15.5 32.7 %collective-permute-start = (bf16[256,256]{1,0:T(8,128)(2,1)}, bf16[256,256]{1,0:T(8,128)(2,1)}, u32[]{:S(2)}, u32[]{:S(2)}) collective-permute-start(bf16[256,256]{1,0:T(8,128)(2,1)} %bitcast.6), channel_id=1, source_target_pairs={{0,1},{1,2},{2,3},{3,4},{4,5},{5,6},{6,7},{7,8},{8,9},{9,10},{10,1... | collective-permute-start | bytes 393224 | tf_op jit(solution)/shard_map/ppermute | solution.py:18
  21.0 7.1 %all-to-all-start.1 = ((bf16[128,2,2048]{2,0,1:T(8,128)(2,1)}), bf16[128,2,2048]{2,0,1:T(8,128)(2,1)S(1)}, u32[]{:S(2)}, u32[]{:S(2)}) async-start(bf16[128,2,2048]{2,0,1:T(8,128)(2,1)} %bitcast.144), calls=%async_computation.1 | async-start | bytes 2097152 | tf_op jit(solution)/shard_map/all_to_all | solution.py:56
  28.1 10.0 %all-to-all-start.3 = ((bf16[128,2,2048]{2,0,1:T(8,128)(2,1)}), bf16[128,2,2048]{2,0,1:T(8,128)(2,1)}, u32[]{:S(2)}, u32[]{:S(2)}) async-start(bf16[128,2,2048]{2,0,1:T(8,128)(2,1)} %bitcast.143), calls=%async_computation.3 | async-start | bytes 2097152 | tf_op jit(solution)/shard_map/all_to_all | solution.py:57
  38.0 10.2 %all-to-all-start.4 = ((bf16[128,2,16]{0,2,1:T(8,128)(2,1)}), bf16[128,2,16]{0,2,1:T(8,128)(2,1)S(1)}, u32[]{:S(2)}, u32[]{:S(2)}) async-start(bf16[128,2,16]{0,2,1:T(8,128)(2,1)} %bitcast.15), calls=%async_computation.4 | async-start | bytes 16384 | tf_op jit(solution)/shard_map/all_to_all | solution.py:58
  45.4 2.0 %copy-start = (f32[2,256,256,8]{2,1,3,0:T(8,128)}, f32[2,256,256,8]{2,1,3,0:T(8,128)S(1)}, u32[]{:S(2)}) copy-start(f32[2,256,256,8]{2,1,3,0:T(8,128)S(1)} %get-tuple-element.23) | copy-start | bytes 12582916
  49.3 3.4 %copy-start.1 = (f32[2,256,256,8]{2,1,3,0:T(8,128)S(1)}, f32[2,256,256,8]{2,1,3,0:T(8,128)}, u32[]{:S(2)}) copy-start(f32[2,256,256,8]{2,1,3,0:T(8,128)} %copy-done) | copy-start | bytes 12582916
  50.0 3.7 %copy-start.2 = (f32[2,256,256,8]{2,1,3,0:T(8,128)}, f32[2,256,256,8]{2,1,3,0:T(8,128)S(1)}, u32[]{:S(2)}) copy-start(f32[2,256,256,8]{2,1,3,0:T(8,128)S(1)} %get-tuple-element.25) | copy-start | bytes 12582916
  56.8 1.3 %copy-start.3 = (bf16[2,8,256,256]{2,3,1,0:T(8,128)(2,1)}, bf16[2,8,256,256]{2,3,1,0:T(8,128)(2,1)S(1)}, u32[]{:S(2)}) copy-start(bf16[2,8,256,256]{2,3,1,0:T(8,128)(2,1)S(1)} %fusion.3) | copy-start | bytes 6291460
  61.4 5.1 %copy-start.5 = (f32[2,8,256,128]{3,2,1,0:T(8,128)S(1)}, f32[2,8,256,128]{3,2,1,0:T(8,128)}, u32[]{:S(2)}) copy-start(f32[2,8,256,128]{3,2,1,0:T(8,128)} %fusion.18) | copy-start | bytes 6291460
  65.1 2.5 %copy-start.7 = (f32[2,256,128,1]{1,2,3,0:T(8,128)S(1)}, f32[2,256,128,1]{1,2,3,0:T(8,128)}, u32[]{:S(2)}) copy-start(f32[2,256,128,1]{1,2,3,0:T(8,128)} %fusion.8) | copy-start | bytes 786436
  65.1 8.7 %copy-start.4 = (bf16[2,8,256,256]{2,3,1,0:T(8,128)(2,1)S(1)}, bf16[2,8,256,256]{2,3,1,0:T(8,128)(2,1)}, u32[]{:S(2)}) copy-start(bf16[2,8,256,256]{2,3,1,0:T(8,128)(2,1)} %copy-done.3) | copy-start | bytes 6291460
  67.6 14.9 %collective-permute-start.3 = (f32[256,256]{0,1:T(8,128)S(1)}, f32[256,256]{0,1:T(8,128)S(1)}, u32[]{:S(2)}, u32[]{:S(2)}) collective-permute-start(f32[256,256]{0,1:T(8,128)S(1)} %bitcast.166), channel_id=1, source_target_pairs={{1,0},{2,1},{3,2},{4,3},{5,4},{6,5},{7,6},{8,7},{9,8},{10,9},{11,1... | collective-permute-start | bytes 786440 | tf_op jit(solution)/shard_map/ppermute | solution.py:18
  71.6 15.8 %collective-permute-start.2 = (f32[256,256]{0,1:T(8,128)}, f32[256,256]{0,1:T(8,128)S(1)}, u32[]{:S(2)}, u32[]{:S(2)}) collective-permute-start(f32[256,256]{0,1:T(8,128)} %bitcast.34), channel_id=1, source_target_pairs={{1,0},{2,1},{3,2},{4,3},{5,4},{6,5},{7,6},{8,7},{9,8},{10,9},{11,1... | collective-permute-start | bytes 786440 | tf_op jit(solution)/shard_map/ppermute | solution.py:18
where the time goes:
time: 93.3 us; the launch traced here: 92.3 us
  starting transfers between devices  31.8 us (34%)
  local copies, waits for them, and re-layouts  26 us (28%)
  matrix products  14.8 us (16%)
  blocking collectives  12.5 us (13%)
  other arithmetic  6.21 us (7%)
  between operations  1.06 us (1%)
    unnamed x26, local copies, waits for them, and re-layouts  13.3 us
    ppermute x4, starting transfers between devices, shifted(): return lax.ppermute(shard, axis, pairs)  12.4 us
    dot_general x2, matrix products, on_device(): jnp.einsum('tkgd,ukd->kgtu', grad_heads, value_heads, preferred_element_t...  4.82 us
    all_to_all x1, blocking collectives, on_device(): lax.all_to_all(query_low, 'head', split_axis=0, concat_axis=1, tiled=True)  4.79 us
    all_to_all x1, starting transfers between devices, on_device(): lax.all_to_all(output_gradient, 'head', split_axis=1, concat_axis=0, tile...  4.41 us
    all_to_all x1, starting transfers between devices, on_device(): lax.all_to_all(queries, 'head', split_axis=1, concat_axis=0, tiled=True)  4.15 us
    all_to_all x1, starting transfers between devices, on_device(): lax.all_to_all(values, 'head', split_axis=1, concat_axis=0, tiled=True)  4.04 us
    all_to_all x1, blocking collectives, on_device(): lax.all_to_all(value_total.astype(jnp.bfloat16), 'head', split_axis=0, co...  3.86 us
  transfers between devices with their start and end apart: 9, of which 0 were waited for; matrix products, arithmetic and copies ran while one was open for 35% of the time, Pallas kernels for 0%

commit v1 on v0

v1 whole, which is shorter than its diff:
```python
import functools
import math

import jax
import jax.numpy as jnp
from jax import lax
from jax.experimental import pallas as pl
from jax.experimental.pallas import tpu as pltpu
from jax.sharding import PartitionSpec as P

HEAD_SIZE = 128
KEY_VALUE_HEADS = 4
WINDOW_SHARDS = 2
fill_value = -1e30
MESH = pl.DeviceIdType.MESH
NT = (((1,), (1,)), ((), ()))
TN = (((0,), (0,)), ((), ()))


def kernel(
    n_ctx, n_head, group, kv_heads,
    doc_ref, q_hbm, k_hbm, v_hbm, o_hbm, g_hbm,
    dq_hbm, dk_hbm, dv_hbm,
    qv, gv, ov, dqv, kw, vw, dlt, bias, p_buf, s_buf,
    own_dk, own_dv, send_dk, send_dv, got_dk, got_dv, out_dk, out_dv,
    in_sem, kv_sem, out_sem, fwd_send, fwd_recv, ret_send, ret_recv,
):
    d = HEAD_SIZE
    rows = q_hbm.shape[0]
    wide = group * d
    count = n_ctx * n_head
    back = WINDOW_SHARDS
    me = lax.axis_index("ctx") * n_head + lax.axis_index("head")
    scale = d ** -0.5

    def device(index):
        return {"ctx": index // n_head, "head": lax.rem(index, n_head)}

    def load(g):
        cols = pl.ds(g * wide, wide)
        return [
            pltpu.make_async_copy(g_hbm.at[:, cols], gv.at[g], in_sem.at[0, g]),
            pltpu.make_async_copy(o_hbm.at[:, cols], ov.at[g], in_sem.at[1, g]),
            pltpu.make_async_copy(q_hbm.at[:, cols], qv.at[g], in_sem.at[2, g]),
        ]

    def load_kv(g):
        cols = pl.ds(g * d, d)
        here = pl.ds(back * rows, rows)
        return [
            pltpu.make_async_copy(k_hbm.at[:, cols], kw.at[g, here], kv_sem.at[0, g]),
            pltpu.make_async_copy(v_hbm.at[:, cols], vw.at[g, here], kv_sem.at[1, g]),
        ]

    def forward(g, j):
        cols = pl.ds(pl.multiple_of(g * d, d), d)
        there = pl.ds((back - j) * rows, rows)
        target = device(lax.rem(me + j, count))
        return [
            pltpu.make_async_remote_copy(
                src_ref=src.at[:, cols], dst_ref=dst.at[g, there],
                send_sem=fwd_send.at[j - 1, i, g], recv_sem=fwd_recv.at[j - 1, i, g],
                device_id=target, device_id_type=MESH,
            )
            for i, (src, dst) in enumerate(((k_hbm, kw), (v_hbm, vw)))
        ]

    def give_back(g, j):
        there = pl.ds((back - j) * rows, rows)
        target = device(lax.rem(me - j + count, count))
        return [
            pltpu.make_async_remote_copy(
                src_ref=src.at[g, there], dst_ref=dst.at[j - 1, g],
                send_sem=ret_send.at[j - 1, i, g], recv_sem=ret_recv.at[j - 1, i, g],
                device_id=target, device_id_type=MESH,
            )
            for i, (src, dst) in enumerate(((send_dk, got_dk), (send_dv, got_dv)))
        ]

    for g in range(kv_heads):
        for copy in load(g) + load_kv(g):
            copy.start()

    barrier = pltpu.get_barrier_semaphore()
    peers = jnp.int32(0)
    for j in range(1, back + 1):
        @pl.when(me + j < count)
        def _():
            pl.semaphore_signal(
                barrier, inc=1, device_id=device(me + j), device_id_type=MESH
            )

        @pl.when(me - j >= 0)
        def _():
            pl.semaphore_signal(
                barrier, inc=1, device_id=device(me - j), device_id_type=MESH
            )

        peers = peers + (me + j < count).astype(jnp.int32) + (me - j >= 0).astype(jnp.int32)
    pl.semaphore_wait(barrier, peers)

    for g in range(kv_heads):
        for j in range(1, back + 1):
            @pl.when(me + j < count)
            def _():
                for copy in forward(g, j):
                    copy.start()

    for j in range(1, back + 1):
        @pl.when(me - j < 0)
        def _():
            there = pl.ds((back - j) * rows, rows)
            zero = jnp.zeros((kv_heads, rows, d), jnp.bfloat16)
            kw[:, there, :] = zero
            vw[:, there, :] = zero

        @pl.when(me + j >= count)
        def _():
            zero = jnp.zeros((kv_heads, rows, d), jnp.bfloat16)
            got_dk[j - 1] = zero
            got_dv[j - 1] = zero

    window = (back + 1) * rows
    first = me * rows
    here_t = first + lax.broadcasted_iota(jnp.int32, (8, rows), 1)

    def document(index, state):
        end, start = state
        end = end + doc_ref[index]
        return end, jnp.where(end <= here_t, end, start)

    start = lax.fori_loop(
        0, doc_ref.shape[0], document,
        (jnp.int32(0), jnp.zeros((8, rows), jnp.int32)), unroll=8,
    )[1][:1]
    pos_u = first - back * rows + lax.broadcasted_iota(jnp.int32, (window, rows), 0)
    pos_t = first + lax.broadcasted_iota(jnp.int32, (window, rows), 1)
    allowed = (pos_u <= pos_t) & (pos_u >= start)
    bias[...] = jnp.where(allowed, 0.0, fill_value).astype(jnp.float32)

    lane = lax.broadcasted_iota(jnp.int32, (rows, d), 1)

    def delta_of(g, carry):
        for copy in load(g)[:2]:
            copy.wait()
        for h in range(group):
            cols = slice(h * d, (h + 1) * d)
            product = gv[g, :, cols].astype(jnp.float32) * ov[g, :, cols].astype(jnp.float32)
            delta = jnp.sum(product, axis=1, keepdims=True)
            dlt[g, :, cols] = jnp.where(lane == 0, delta, 0.0).astype(jnp.bfloat16)
        return carry

    lax.fori_loop(0, kv_heads, delta_of, 0)

    minus = jnp.where(
        lax.broadcasted_iota(jnp.int32, (window, d), 1) == 0, -1.0, 0.0
    ).astype(jnp.bfloat16)
    factor = scale * math.log2(math.e)
    step = 2

    def one_group(g, carry):
        load(g)[2].wait()
        for copy in load_kv(g):
            copy.wait()
        for j in range(1, back + 1):
            @pl.when(me - j >= 0)
            def _():
                for copy in forward(g, j):
                    copy.wait_recv()

        k_all = kw[g]
        v_aug = jnp.concatenate([vw[g], minus], axis=1)

        def stack(ref, heads):
            return jnp.concatenate([ref[g, :, h * d : (h + 1) * d] for h in heads], axis=0)

        for pair in range(group // step):
            heads = range(pair * step, (pair + 1) * step)
            q_rows = stack(qv, heads)
            g_aug = jnp.concatenate([stack(gv, heads), stack(dlt, heads)], axis=1)
            scores = lax.dot_general(k_all, q_rows, NT, preferred_element_type=jnp.float32)
            scores = scores * factor + jnp.concatenate([bias[...]] * step, axis=1)
            top = jnp.max(scores, axis=0, keepdims=True)
            grown = jnp.exp2(scores - top)
            inverse = 1.0 / jnp.sum(grown, axis=0, keepdims=True)
            probs = grown * inverse
            cols = slice(pair * step * rows, (pair + 1) * step * rows)
            p_buf[:, cols] = probs.astype(jnp.bfloat16)
            diff = lax.dot_general(v_aug, g_aug, NT, preferred_element_type=jnp.float32)
            s_buf[:, cols] = (probs * diff).astype(jnp.bfloat16)

        dv = jnp.dot(
            p_buf[...], stack(gv, range(group)), preferred_element_type=jnp.float32
        )
        dk = (
            jnp.dot(s_buf[...], stack(qv, range(group)), preferred_element_type=jnp.float32)
            * scale
        )
        far = back * rows
        send_dk[g] = dk[:far].astype(jnp.bfloat16)
        send_dv[g] = dv[:far].astype(jnp.bfloat16)
        for j in range(1, back + 1):
            @pl.when(me - j >= 0)
            def _():
                for copy in give_back(g, j):
                    copy.start()
        own_dk[g] = dk[far:]
        own_dv[g] = dv[far:]
        dq = lax.dot_general(k_all, s_buf[...], TN, preferred_element_type=jnp.float32) * scale
        for h in range(group):
            piece = dq[:, h * rows : (h + 1) * rows]
            dqv[g, :, h * d : (h + 1) * d] = piece.T.astype(jnp.bfloat16)
        put_dq(g).start()
        return carry

    def put_dq(g):
        cols = pl.ds(pl.multiple_of(g * wide, wide), wide)
        return pltpu.make_async_copy(dqv.at[g], dq_hbm.at[:, cols], out_sem.at[g])

    lax.fori_loop(0, kv_heads, one_group, 0)

    for g in range(kv_heads):
        for j in range(1, back + 1):
            @pl.when(me + j < count)
            def _():
                for copy in give_back(g, j):
                    copy.wait_recv()
        cols = slice(g * d, (g + 1) * d)
        dk, dv = own_dk[g], own_dv[g]
        for j in range(back):
            dk = dk + got_dk[j, g].astype(jnp.float32)
            dv = dv + got_dv[j, g].astype(jnp.float32)
        out_dk[:, cols] = dk.astype(jnp.bfloat16)
        out_dv[:, cols] = dv.astype(jnp.bfloat16)
    put_k = pltpu.make_async_copy(out_dk, dk_hbm, out_sem.at[kv_heads])
    put_v = pltpu.make_async_copy(out_dv, dv_hbm, out_sem.at[kv_heads + 1])
    put_k.start()
    put_v.start()
    for g in range(kv_heads):
        put_dq(g).wait()
        for j in range(1, back + 1):
            @pl.when(me + j < count)
            def _():
                for copy in forward(g, j):
                    copy.wait_send()

            @pl.when(me - j >= 0)
            def _():
                for copy in give_back(g, j):
                    copy.wait_send()
    put_k.wait()
    put_v.wait()


def on_device(n_ctx, n_head, queries, keys, values, attn_out, output_gradient, doc_lengths):
    d = HEAD_SIZE
    rows = queries.shape[0]
    kv_heads = keys.shape[1] // d
    group = queries.shape[1] // keys.shape[1]
    wide = group * d
    back = WINDOW_SHARDS
    window = (back + 1) * rows
    low, full = jnp.bfloat16, jnp.float32
    dma = pltpu.SemaphoreType.DMA
    any_space = pl.BlockSpec(memory_space=pl.ANY)
    return pl.pallas_call(
        functools.partial(kernel, n_ctx, n_head, group, kv_heads),
        out_shape=(
            jax.ShapeDtypeStruct(queries.shape, low),
            jax.ShapeDtypeStruct(keys.shape, low),
            jax.ShapeDtypeStruct(values.shape, low),
        ),
        in_specs=[pl.BlockSpec(memory_space=pltpu.SMEM)] + [any_space] * 5,
        out_specs=(any_space,) * 3,
        scratch_shapes=[
            pltpu.VMEM((kv_heads, rows, wide), low),
            pltpu.VMEM((kv_heads, rows, wide), low),
            pltpu.VMEM((kv_heads, rows, wide), low),
            pltpu.VMEM((kv_heads, rows, wide), low),
            pltpu.VMEM((kv_heads, window, d), low),
            pltpu.VMEM((kv_heads, window, d), low),
            pltpu.VMEM((kv_heads, rows, wide), low),
            pltpu.VMEM((window, rows), full),
            pltpu.VMEM((window, group * rows), low),
            pltpu.VMEM((window, group * rows), low),
            pltpu.VMEM((kv_heads, rows, d), full),
            pltpu.VMEM((kv_heads, rows, d), full),
            pltpu.VMEM((kv_heads, back * rows, d), low),
            pltpu.VMEM((kv_heads, back * rows, d), low),
            pltpu.VMEM((back, kv_heads, rows, d), low),
            pltpu.VMEM((back, kv_heads, rows, d), low),
            pltpu.VMEM((rows, kv_heads * d), low),
            pltpu.VMEM((rows, kv_heads * d), low),
            dma((3, kv_heads)),
            dma((2, kv_heads)),
            dma((kv_heads + 2,)),
            dma((back, 2, kv_heads)),
            dma((back, 2, kv_heads)),
            dma((back, 2, kv_heads)),
            dma((back, 2, kv_heads)),
        ],
        compiler_params=pltpu.CompilerParams(collective_id=0, has_side_effects=True),
        name="packed_attention_backward",
    )(doc_lengths, queries, keys, values, attn_out, output_gradient)


def solution(mesh):
    n_ctx, n_head = mesh.shape["ctx"], mesh.shape["head"]
    rows = P(("ctx", "head"), None)
    return jax.shard_map(
        functools.partial(on_device, n_ctx, n_head),
        mesh=mesh,
        in_specs=(rows,) * 5 + (P(),),
        out_specs=(rows,) * 3,
        check_vma=False,
    )
```

time: 93.3 us -> 32.1 us (0.34)
  starting transfers between devices: 31.8 us -> 0 us
  Pallas kernels: 0 us -> 27.1 us
  local copies, waits for them, and re-layouts: 26 us -> 3.93 us
  matrix products: 14.8 us -> 0 us
  blocking collectives: 12.5 us -> 0 us
  other arithmetic: 6.21 us -> 0 us
    pallas_call x0 -> x1, Pallas kernels: none -> 27.1 us  [on_device(): pl.pallas_call(functools.partial(kernel, n_ctx, n_head, group, kv_heads),...]
    all_to_all x5 -> x0, starting transfers between devices: 19.4 us -> none  [the longest x1 4.41 us: on_device(): lax.all_to_all(output_gradient, 'head', split_axis=1, concat_axis=0, tile...]
    dot_general x10 -> x0, matrix products: 14.8 us -> none  [the longest x2 4.82 us: on_device(): jnp.einsum('tkgd,ukd->kgtu', grad_heads, value_heads, preferred_element_t...]
    all_to_all x3 -> x0, blocking collectives: 12.5 us -> none  [the longest x1 4.79 us: on_device(): lax.all_to_all(query_low, 'head', split_axis=0, concat_axis=1, tiled=True)]
    ppermute x4 -> x0, starting transfers between devices: 12.4 us -> none  [shifted(): return lax.ppermute(shard, axis, pairs)]
    unnamed x26 -> x7, local copies, waits for them, and re-layouts: 13.3 us -> 3.93 us
    all_to_all x7 -> x0, local copies, waits for them, and re-layouts: 5.17 us -> none  [the longest x1 2.31 us: on_device(): lax.all_to_all(queries, 'head', split_axis=1, concat_axis=0, tiled=True)]
    reduce_sum x4 -> x0, other arithmetic: 3.68 us -> none  [the longest x2 1.69 us: on_device(): tile_sum = jnp.sum(jnp.exp(masked - tile_max[..., None]), axis=-1)]
  transfers between devices with their start and end apart: 9 -> 0, of which waited for: 0 -> 0; matrix products, arithmetic and copies ran while one was open for 35% -> 0% of each run, Pallas kernels for 0% -> 0%
where the time goes in v1:
time: 32.1 us; the launch traced here: 31.7 us
  Pallas kernels  27.1 us (84%)
  local copies, waits for them, and re-layouts  3.93 us (12%)
  between operations  0.65 us (2%)
    pallas_call x1, Pallas kernels, on_device(): pl.pallas_call(functools.partial(kernel, n_ctx, n_head, group, kv_heads),...  27.1 us
    unnamed x7, local copies, waits for them, and re-layouts  3.93 us

profile of v1, /device:TPU:17, one launch (start us, length us, event | category | flops | bytes accessed | tf_op | source)
XLA Modules:
  0.0 31.7 jit_solution(8305850973355042643)
XLA Ops:
  0.6 27.1 %packed_attention_backward.1 = (bf16[128,4096]{1,0:T(8,128)(2,1)}, bf16[128,512]{1,0:T(8,128)(2,1)}, bf16[128,512]{1,0:T(8,128)(2,1)}) custom-call(s32[32]{0:T(128)} %doc_ref.1, bf16[128,4096]{1,0:T(8,128)(2,1)} %q_hbm.1, bf16[128,512]{1,0:T(8,128)(2,1)} %k_hbm.1, bf16[128,512]{1,0:T(8,128)(2,1)} %v_hbm.1, bf16[128,4096]{1,0:T(8,128)(2,1)} %o_hbm.1, ...), custom_call_target="tpu_custom_call" | custom-call | tf_op jit(solution)/shard_map/packed_attention_backward/pallas_call | solution.py:266
  27.7 0.0 copy-start.1
  27.7 2.3 %copy.12 = bf16[128,4096]{1,0:T(8,128)(2,1)} copy(bf16[128,4096]{1,0:T(8,128)(2,1)} %get-tuple-element.6) | data formatting | bytes 2097152
  30.1 0.0 copy-done.1
  30.1 0.0 copy-start
  30.1 0.7 %copy.13 = bf16[128,512]{1,0:T(8,128)(2,1)} copy(bf16[128,512]{1,0:T(8,128)(2,1)S(1)} %copy-done.1) | data formatting | bytes 262144
  30.7 0.3 copy-done
  31.0 0.7 %copy.14 = bf16[128,512]{1,0:T(8,128)(2,1)} copy(bf16[128,512]{1,0:T(8,128)(2,1)S(1)} %copy-done) | data formatting | bytes 262144
Async XLA Ops:
  27.7 2.3 %copy-start.1 = (bf16[128,512]{1,0:T(8,128)(2,1)S(1)}, bf16[128,512]{1,0:T(8,128)(2,1)}, u32[]{:S(2)}) copy-start(bf16[128,512]{1,0:T(8,128)(2,1)} %get-tuple-element.7) | copy-start | bytes 393220
  30.1 1.0 %copy-start = (bf16[128,512]{1,0:T(8,128)(2,1)S(1)}, bf16[128,512]{1,0:T(8,128)(2,1)}, u32[]{:S(2)}) copy-start(bf16[128,512]{1,0:T(8,128)(2,1)} %get-tuple-element.8) | copy-start | bytes 393220

commit v2 on v1

v2 whole, which is shorter than its diff:
```python
import functools
import math

import jax
import jax.numpy as jnp
from jax import lax
from jax.experimental import pallas as pl
from jax.experimental.pallas import tpu as pltpu
from jax.sharding import PartitionSpec as P

HEAD_SIZE = 128
fill_value = -1e30
MESH = pl.DeviceIdType.MESH
NT = (((1,), (1,)), ((), ()))
TN = (((0,), (0,)), ((), ()))


def kernel(
    n_ctx, group, mine_count,
    doc_ref, q_hbm, k_hbm, v_hbm, o_hbm, g_hbm,
    dq_out, dk_out, dv_out,
    q_buf, g_buf, g_all, o_all, d_buf, d_send,
    kw, vw, bias, p_buf, s_buf, acc_k, acc_v, own_k, own_v,
    send_k, send_v, part_k, part_v, next_k, next_v, dq_buf, dq_got,
    in_sem, fwd_send, fwd_recv, ret_send, ret_recv, chip_send, chip_recv,
):
    d = HEAD_SIZE
    rows = q_hbm.shape[0]
    wide = group * d
    window = 3 * rows
    ctx = lax.axis_index("ctx")
    me = lax.axis_index("head")
    other = 1 - me
    scale = d ** -0.5
    has_next = ctx + 1 < n_ctx
    has_back = ctx >= 1
    following = lax.rem(ctx + 1, n_ctx)
    previous = lax.rem(ctx + n_ctx - 1, n_ctx)

    def block(index, width):
        return pl.ds(pl.multiple_of(index * width, width), width)

    def remote(src, dst, send, recv, where, head):
        return pltpu.make_async_remote_copy(
            src_ref=src, dst_ref=dst, send_sem=send, recv_sem=recv,
            device_id={"ctx": where, "head": head}, device_id_type=MESH,
        )

    def load_mine(i):
        cols = block(me * mine_count + i, d)
        here = block(2 + me, rows)
        return [
            pltpu.make_async_copy(
                q_hbm.at[:, block(me * mine_count + i, wide)], q_buf.at[i, me], in_sem.at[0, i]
            ),
            pltpu.make_async_copy(
                g_hbm.at[:, block(me * mine_count + i, wide)], g_buf.at[i, me], in_sem.at[5, i]
            ),
            pltpu.make_async_copy(k_hbm.at[:, cols], kw.at[i, here], in_sem.at[1, i]),
            pltpu.make_async_copy(v_hbm.at[:, cols], vw.at[i, here], in_sem.at[2, i]),
        ]

    def load_all(g):
        cols = block(g, wide)
        return [
            pltpu.make_async_copy(g_hbm.at[:, cols], g_all.at[g], in_sem.at[3, g]),
            pltpu.make_async_copy(o_hbm.at[:, cols], o_all.at[g], in_sem.at[4, g]),
        ]

    def forward(i, source, head):
        cols = block(head * mine_count + i, d)
        return [
            remote(
                src.at[:, cols], dst.at[i, block(source, rows)],
                fwd_send.at[head, x, i], fwd_recv.at[source, x, i], following, head,
            )
            for x, (src, dst) in enumerate(((k_hbm, kw), (v_hbm, vw)))
        ]

    def give_back(i, source, head):
        return [
            remote(
                src.at[i, head], dst.at[source * mine_count + i],
                ret_send.at[head, x, i], ret_recv.at[source, x, i], previous, head,
            )
            for x, (src, dst) in enumerate(((send_k, next_k), (send_v, next_v)))
        ]

    def across(i, source):
        theirs = (1 - source) * mine_count + i
        cols = block(theirs, d)
        return [
            remote(
                src, dst, chip_send.at[x, i], chip_recv.at[x, i], ctx, 1 - source
            )
            for x, (src, dst) in enumerate((
                (k_hbm.at[:, cols], kw.at[i, block(2 + source, rows)]),
                (v_hbm.at[:, cols], vw.at[i, block(2 + source, rows)]),
                (q_hbm.at[:, block(theirs, wide)], q_buf.at[i, source]),
                (g_hbm.at[:, block(theirs, wide)], g_buf.at[i, source]),
                (d_send.at[i], d_buf.at[i, source]),
                (dq_buf.at[i, 1 - source], dq_got.at[i]),
                (send_k.at[i, 2], part_k.at[i]),
                (send_v.at[i, 2], part_v.at[i]),
            ))
        ]

    barrier = pltpu.get_barrier_semaphore()

    def greet(where, head):
        pl.semaphore_signal(
            barrier, inc=1, device_id={"ctx": where, "head": head}, device_id_type=MESH
        )

    greet(ctx, other)
    for head in range(2):
        @pl.when(has_next)
        def _():
            greet(following, head)

        @pl.when(has_back)
        def _():
            greet(previous, head)

    for i in range(mine_count):
        for copy in load_mine(i):
            copy.start()
    for g in range(2 * mine_count):
        for copy in load_all(g):
            copy.start()

    pl.semaphore_wait(
        barrier, 1 + 2 * has_next.astype(jnp.int32) + 2 * has_back.astype(jnp.int32)
    )

    for i in range(mine_count):
        @pl.when(has_next)
        def _():
            for head in range(2):
                for copy in forward(i, me, head):
                    copy.start()

        for copy in across(i, me)[:4]:
            copy.start()

    @pl.when(jnp.logical_not(has_back))
    def _():
        zero = jnp.zeros((mine_count, 2 * rows, d), jnp.bfloat16)
        kw[:, : 2 * rows, :] = zero
        vw[:, : 2 * rows, :] = zero

    @pl.when(jnp.logical_not(has_next))
    def _():
        next_k[...] = jnp.zeros(next_k.shape, jnp.bfloat16)
        next_v[...] = jnp.zeros(next_v.shape, jnp.bfloat16)

    lane = lax.broadcasted_iota(jnp.int32, (rows, d), 1)

    def delta_of(g):
        for copy in load_all(g):
            copy.wait()
        total = jnp.zeros((rows, d), jnp.float32)
        for h in range(group):
            cols = slice(h * d, (h + 1) * d)
            product = g_all[g, :, cols].astype(jnp.float32) * o_all[g, :, cols].astype(jnp.float32)
            total = jnp.where(lane == h, jnp.sum(product, axis=1, keepdims=True), total)
        return total.astype(jnp.bfloat16)

    for i in range(mine_count):
        d_send[i] = delta_of(other * mine_count + i)
        across(i, me)[4].start()

    for token_block in range(2):
        first = (2 * ctx + token_block) * rows
        here_t = first + lax.broadcasted_iota(jnp.int32, (8, rows), 1)

        def document(index, state):
            end, start = state
            end = end + doc_ref[index]
            return end, jnp.where(end <= here_t, end, start)

        start = lax.fori_loop(
            0, doc_ref.shape[0], document,
            (jnp.int32(0), jnp.zeros((8, rows), jnp.int32)), unroll=8,
        )[1][:1]
        pos_u = first - 2 * rows + lax.broadcasted_iota(jnp.int32, (window, rows), 0)
        pos_t = first + lax.broadcasted_iota(jnp.int32, (window, rows), 1)
        allowed = (pos_u <= pos_t) & (pos_u >= start)
        bias[token_block] = jnp.where(allowed, 0.0, fill_value).astype(jnp.float32)

    for i in range(mine_count):
        d_buf[i, me] = delta_of(me * mine_count + i)

    minus = jnp.full((window, d), -1.0, jnp.bfloat16)
    factor = scale * math.log2(math.e)
    step = 2

    def unit(i, token_block):
        span = slice(token_block * rows, token_block * rows + window)
        k_all = kw[i, span]
        v_aug = jnp.concatenate([vw[i, span], minus], axis=1)

        def stack(ref, heads):
            return jnp.concatenate(
                [ref[i, token_block, :, h * d : (h + 1) * d] for h in heads], axis=0
            )

        for pair in range(group // step):
            heads = range(pair * step, (pair + 1) * step)
            q_rows = stack(q_buf, heads)
            deltas = d_buf[i, token_block]
            zero = jnp.zeros_like(deltas)
            d_rows = jnp.concatenate([jnp.where(lane == h, deltas, zero) for h in heads], axis=0)
            g_aug = jnp.concatenate([stack(g_buf, heads), d_rows], axis=1)
            scores = lax.dot_general(k_all, q_rows, NT, preferred_element_type=jnp.float32)
            scores = scores * factor + jnp.concatenate([bias[token_block]] * step, axis=1)
            top = jnp.max(scores, axis=0, keepdims=True)
            grown = jnp.exp2(scores - top)
            inverse = 1.0 / jnp.sum(grown, axis=0, keepdims=True)
            probs = grown * inverse
            cols = slice(pair * step * rows, (pair + 1) * step * rows)
            p_buf[:, cols] = probs.astype(jnp.bfloat16)
            diff = lax.dot_general(v_aug, g_aug, NT, preferred_element_type=jnp.float32)
            s_buf[:, cols] = (probs * diff).astype(jnp.bfloat16)

        acc_v[span, :] += jnp.dot(
            p_buf[...], stack(g_buf, range(group)), preferred_element_type=jnp.float32
        )
        acc_k[span, :] += (
            jnp.dot(s_buf[...], stack(q_buf, range(group)), preferred_element_type=jnp.float32)
            * scale
        )

    def query_part(i, token_block):
        span = slice(token_block * rows, token_block * rows + window)
        dq = lax.dot_general(
            kw[i, span], s_buf[...], TN, preferred_element_type=jnp.float32
        ) * scale
        for h in range(group):
            piece = dq[:, h * rows : (h + 1) * rows].T.astype(jnp.bfloat16)
            dq_buf[i, token_block, :, h * d : (h + 1) * d] = piece

        @pl.when(me != token_block)
        def _():
            across(i, me)[5].start()

    def finish(i, head):
        for acc, send in ((acc_k, send_k), (acc_v, send_v)):
            send[i, head] = acc[head * rows : (head + 1) * rows].astype(jnp.bfloat16)

        @pl.when(has_back)
        def _():
            for copy in give_back(i, me, head):
                copy.start()

    def one_group(i):
        for copy in load_mine(i):
            copy.wait()
        for copy in across(i, other)[:5]:
            copy.wait_recv()

        @pl.when(has_back)
        def _():
            for source in range(2):
                for copy in forward(i, source, me):
                    copy.wait_recv()

        acc_k[...] = jnp.zeros(acc_k.shape, jnp.float32)
        acc_v[...] = jnp.zeros(acc_v.shape, jnp.float32)
        unit(i, 0)
        finish(i, 0)
        query_part(i, 0)
        unit(i, 1)
        finish(i, 1)
        for acc, send, own in ((acc_k, send_k, own_k), (acc_v, send_v, own_v)):
            send[i, 2] = acc[block(2 + other, rows), :].astype(jnp.bfloat16)
            own[i] = acc[block(2 + me, rows), :]
        for copy in across(i, me)[6:]:
            copy.start()
        query_part(i, 1)

    for i in range(mine_count):
        one_group(i)

    for i in range(mine_count):
        for copy in across(i, other)[5:]:
            copy.wait_recv()

        @pl.when(has_next)
        def _():
            for source in range(2):
                for copy in give_back(i, source, me):
                    copy.wait_recv()

        dq_out[:, block(other * mine_count + i, wide)] = dq_got[i]
        dq_out[:, block(me * mine_count + i, wide)] = dq_buf[i, me]
        for own, part, late, out in (
            (own_k, part_k, next_k, dk_out), (own_v, part_v, next_v, dv_out)
        ):
            g = me * mine_count + i
            total = own[i] + late[g].astype(jnp.float32)
            out[:, block(g, d)] = total.astype(jnp.bfloat16)
            g = other * mine_count + i
            total = part[i].astype(jnp.float32) + late[g].astype(jnp.float32)
            out[:, block(g, d)] = total.astype(jnp.bfloat16)

    for i in range(mine_count):
        for copy in across(i, me):
            copy.wait_send()

        @pl.when(has_next)
        def _():
            for head in range(2):
                for copy in forward(i, me, head):
                    copy.wait_send()

        @pl.when(has_back)
        def _():
            for head in range(2):
                for copy in give_back(i, me, head):
                    copy.wait_send()


def on_device(n_ctx, n_head, queries, keys, values, attn_out, output_gradient, doc_lengths):
    d = HEAD_SIZE
    rows = queries.shape[0]
    kv_heads = keys.shape[1] // d
    group = queries.shape[1] // keys.shape[1]
    wide = group * d
    mine = kv_heads // n_head
    low, full = jnp.bfloat16, jnp.float32
    dma = pltpu.SemaphoreType.DMA
    any_space = pl.BlockSpec(memory_space=pl.ANY)
    return pl.pallas_call(
        functools.partial(kernel, n_ctx, group, mine),
        out_shape=(
            pltpu.VMEM(queries.shape, low),
            pltpu.VMEM(keys.shape, low),
            pltpu.VMEM(values.shape, low),
        ),
        in_specs=[pl.BlockSpec(memory_space=pltpu.SMEM)] + [any_space] * 5,
        out_specs=(pl.BlockSpec(memory_space=pltpu.VMEM),) * 3,
        scratch_shapes=[
            pltpu.VMEM((mine, 2, rows, wide), low),
            pltpu.VMEM((mine, 2, rows, wide), low),
            pltpu.VMEM((kv_heads, rows, wide), low),
            pltpu.VMEM((kv_heads, rows, wide), low),
            pltpu.VMEM((mine, 2, rows, d), low),
            pltpu.VMEM((mine, rows, d), low),
            pltpu.VMEM((mine, 4 * rows, d), low),
            pltpu.VMEM((mine, 4 * rows, d), low),
            pltpu.VMEM((2, 3 * rows, rows), full),
            pltpu.VMEM((3 * rows, group * rows), low),
            pltpu.VMEM((3 * rows, group * rows), low),
            pltpu.VMEM((4 * rows, d), full),
            pltpu.VMEM((4 * rows, d), full),
            pltpu.VMEM((mine, rows, d), full),
            pltpu.VMEM((mine, rows, d), full),
            pltpu.VMEM((mine, 3, rows, d), low),
            pltpu.VMEM((mine, 3, rows, d), low),
            pltpu.VMEM((mine, rows, d), low),
            pltpu.VMEM((mine, rows, d), low),
            pltpu.VMEM((kv_heads, rows, d), low),
            pltpu.VMEM((kv_heads, rows, d), low),
            pltpu.VMEM((mine, 2, rows, wide), low),
            pltpu.VMEM((mine, rows, wide), low),
            dma((6, kv_heads)),
            dma((2, 2, mine)),
            dma((2, 2, mine)),
            dma((2, 2, mine)),
            dma((2, 2, mine)),
            dma((8, mine)),
            dma((8, mine)),
        ],
        compiler_params=pltpu.CompilerParams(collective_id=0, has_side_effects=True),
        name="packed_attention_backward",
    )(doc_lengths, queries, keys, values, attn_out, output_gradient)


def solution(mesh):
    n_ctx, n_head = mesh.shape["ctx"], mesh.shape["head"]
    rows = P(("ctx", "head"), None)
    return jax.shard_map(
        functools.partial(on_device, n_ctx, n_head),
        mesh=mesh,
        in_specs=(rows,) * 5 + (P(),),
        out_specs=(rows,) * 3,
        check_vma=False,
    )
```

time: 32.1 us -> 23.6 us (0.74)
  the two profiles are of different devices: /device:TPU:17 before, /device:TPU:23 now
where the time goes in v2:
time: 23.6 us; the launch traced here: 23.4 us
  Pallas kernels  20.5 us (87%)
  local copies, waits for them, and re-layouts  2.28 us (10%)
  between operations  0.64 us (3%)
    pallas_call x1, Pallas kernels, on_device(): pl.pallas_call(functools.partial(kernel, n_ctx, group, mine), out_shape=(...  20.5 us
    unnamed x3, local copies, waits for them, and re-layouts  2.28 us

profile of v2, /device:TPU:23, one launch (start us, length us, event | category | flops | bytes accessed | tf_op | source)
XLA Modules:
  0.0 23.4 jit_solution(7227668883955617940)
XLA Ops:
  0.6 20.5 %packed_attention_backward.1 = (bf16[128,4096]{1,0:T(8,128)(2,1)S(1)}, bf16[128,512]{1,0:T(8,128)(2,1)S(1)}, bf16[128,512]{1,0:T(8,128)(2,1)S(1)}) custom-call(s32[32]{0:T(128)} %doc_ref.1, bf16[128,4096]{1,0:T(8,128)(2,1)} %q_hbm.1, bf16[128,512]{1,0:T(8,128)(2,1)} %k_hbm.1, bf16[128,512]{1,0:T(8,128)(2,1)} %v_hbm.1, bf16[128,4096]{1,0:T(8,128)(2,1)} %o_hbm.1, ...), custom_call_target="tpu_custom_call" | custom-call | tf_op jit(solution)/shard_map/packed_attention_backward/pallas_call | solution.py:334
  21.1 1.0 %copy.12 = bf16[128,4096]{1,0:T(8,128)(2,1)} copy(bf16[128,4096]{1,0:T(8,128)(2,1)S(1)} %get-tuple-element.3) | data formatting | bytes 2097152
  22.1 0.7 %copy.13 = bf16[128,512]{1,0:T(8,128)(2,1)} copy(bf16[128,512]{1,0:T(8,128)(2,1)S(1)} %get-tuple-element.4) | data formatting | bytes 262144
  22.7 0.7 %copy.14 = bf16[128,512]{1,0:T(8,128)(2,1)} copy(bf16[128,512]{1,0:T(8,128)(2,1)S(1)} %get-tuple-element.5) | data formatting | bytes 262144

commit v3 on v2

--- a/solution.py
+++ b/solution.py
@@ -20,7 +20,7 @@
     doc_ref, q_hbm, k_hbm, v_hbm, o_hbm, g_hbm,
     dq_out, dk_out, dv_out,
     q_buf, g_buf, g_all, o_all, d_buf, d_send,
-    kw, vw, bias, p_buf, s_buf, acc_k, acc_v, own_k, own_v,
+    kw, vw, bias, p_buf, s_buf, acc_k, acc_v, near_k, near_v, own_k, own_v,
     send_k, send_v, part_k, part_v, next_k, next_v, dq_buf, dq_got,
     in_sem, fwd_send, fwd_recv, ret_send, ret_recv, chip_send, chip_recv,
 ):
@@ -200,18 +200,13 @@
         k_all = kw[i, span]
         v_aug = jnp.concatenate([vw[i, span], minus], axis=1)
 
-        def stack(ref, heads):
-            return jnp.concatenate(
-                [ref[i, token_block, :, h * d : (h + 1) * d] for h in heads], axis=0
-            )
-
         for pair in range(group // step):
             heads = range(pair * step, (pair + 1) * step)
-            q_rows = stack(q_buf, heads)
+            q_rows = stack(q_buf, i, token_block, heads)
             deltas = d_buf[i, token_block]
             zero = jnp.zeros_like(deltas)
             d_rows = jnp.concatenate([jnp.where(lane == h, deltas, zero) for h in heads], axis=0)
-            g_aug = jnp.concatenate([stack(g_buf, heads), d_rows], axis=1)
+            g_aug = jnp.concatenate([stack(g_buf, i, token_block, heads), d_rows], axis=1)
             scores = lax.dot_general(k_all, q_rows, NT, preferred_element_type=jnp.float32)
             scores = scores * factor + jnp.concatenate([bias[token_block]] * step, axis=1)
             top = jnp.max(scores, axis=0, keepdims=True)
@@ -219,22 +214,60 @@
             inverse = 1.0 / jnp.sum(grown, axis=0, keepdims=True)
             probs = grown * inverse
             cols = slice(pair * step * rows, (pair + 1) * step * rows)
-            p_buf[:, cols] = probs.astype(jnp.bfloat16)
+            p_buf[i, token_block, :, cols] = probs.astype(jnp.bfloat16)
             diff = lax.dot_general(v_aug, g_aug, NT, preferred_element_type=jnp.float32)
-            s_buf[:, cols] = (probs * diff).astype(jnp.bfloat16)
-
-        acc_v[span, :] += jnp.dot(
-            p_buf[...], stack(g_buf, range(group)), preferred_element_type=jnp.float32
+            s_buf[i, token_block, :, cols] = (probs * diff).astype(jnp.bfloat16)
+
+    def stack(ref, i, token_block, heads):
+        return jnp.concatenate(
+            [ref[i, token_block, :, h * d : (h + 1) * d] for h in heads], axis=0
         )
-        acc_k[span, :] += (
-            jnp.dot(s_buf[...], stack(q_buf, range(group)), preferred_element_type=jnp.float32)
-            * scale
+
+    def key_sum(buf, ref, i, token_block, low, high):
+        return jnp.dot(
+            buf[i, token_block, low:high], stack(ref, i, token_block, range(group)),
+            preferred_element_type=jnp.float32,
         )
+
+    def far_part(i, token_block):
+        for buf, ref, send, carry, factor_out in (
+            (s_buf, q_buf, send_k, acc_k, scale), (p_buf, g_buf, send_v, acc_v, None)
+        ):
+            total = key_sum(buf, ref, i, token_block, 0, (2 - token_block) * rows)
+            if token_block == 0:
+                carry[...] = total[rows:]
+                total = total[:rows]
+            else:
+                total = total + carry[...]
+            if factor_out is not None:
+                total = total * factor_out
+            send[i, token_block] = total.astype(jnp.bfloat16)
+
+        @pl.when(has_back)
+        def _():
+            for copy in give_back(i, me, token_block):
+                copy.start()
+
+    def near_part(i):
+        for buf, ref, send, own, near, factor_out in (
+            (s_buf, q_buf, send_k, own_k, near_k, scale),
+            (p_buf, g_buf, send_v, own_v, near_v, None),
+        ):
+            early = key_sum(buf, ref, i, 0, 2 * rows, 3 * rows)
+            late = key_sum(buf, ref, i, 1, rows, 3 * rows)
+            if factor_out is not None:
+                early, late = early * factor_out, late * factor_out
+            near[0] = early + late[:rows]
+            near[1] = late[rows:]
+            send[i, 2] = near[other].astype(jnp.bfloat16)
+            own[i] = near[me]
+        for copy in across(i, me)[6:]:
+            copy.start()
 
     def query_part(i, token_block):
         span = slice(token_block * rows, token_block * rows + window)
         dq = lax.dot_general(
-            kw[i, span], s_buf[...], TN, preferred_element_type=jnp.float32
+            kw[i, span], s_buf[i, token_block], TN, preferred_element_type=jnp.float32
         ) * scale
         for h in range(group):
             piece = dq[:, h * rows : (h + 1) * rows].T.astype(jnp.bfloat16)
@@ -243,15 +276,6 @@
         @pl.when(me != token_block)
         def _():
             across(i, me)[5].start()
-
-    def finish(i, head):
-        for acc, send in ((acc_k, send_k), (acc_v, send_v)):
-            send[i, head] = acc[head * rows : (head + 1) * rows].astype(jnp.bfloat16)
-
-        @pl.when(has_back)
-        def _():
-            for copy in give_back(i, me, head):
-                copy.start()
 
     def one_group(i):
         for copy in load_mine(i):
@@ -265,22 +289,16 @@
                 for copy in forward(i, source, me):
                     copy.wait_recv()
 
-        acc_k[...] = jnp.zeros(acc_k.shape, jnp.float32)
-        acc_v[...] = jnp.zeros(acc_v.shape, jnp.float32)
-        unit(i, 0)
-        finish(i, 0)
-        query_part(i, 0)
-        unit(i, 1)
-        finish(i, 1)
-        for acc, send, own in ((acc_k, send_k, own_k), (acc_v, send_v, own_v)):
-            send[i, 2] = acc[block(2 + other, rows), :].astype(jnp.bfloat16)
-            own[i] = acc[block(2 + me, rows), :]
-        for copy in across(i, me)[6:]:
-            copy.start()
-        query_part(i, 1)
+        for token_block in range(2):
+            unit(i, token_block)
+            far_part(i, token_block)
 
     for i in range(mine_count):
         one_group(i)
+    for i in range(mine_count):
+        near_part(i)
+        for token_block in range(2):
+            query_part(i, token_block)
 
     for i in range(mine_count):
         for copy in across(i, other)[5:]:
@@ -321,6 +339,17 @@
                     copy.wait_send()
 
 
+def store_kernel(dq, dk, dv, dq_hbm, dk_hbm, dv_hbm, sem):
+    copies = [
+        pltpu.make_async_copy(src, dst, sem.at[x])
+        for x, (src, dst) in enumerate(((dq, dq_hbm), (dk, dk_hbm), (dv, dv_hbm)))
+    ]
+    for copy in copies:
+        copy.start()
+    for copy in copies:
+        copy.wait()
+
+
 def on_device(n_ctx, n_head, queries, keys, values, attn_out, output_gradient, doc_lengths):
     d = HEAD_SIZE
     rows = queries.shape[0]
@@ -331,7 +360,7 @@
     low, full = jnp.bfloat16, jnp.float32
     dma = pltpu.SemaphoreType.DMA
     any_space = pl.BlockSpec(memory_space=pl.ANY)
-    return pl.pallas_call(
+    results = pl.pallas_call(
         functools.partial(kernel, n_ctx, group, mine),
         out_shape=(
             pltpu.VMEM(queries.shape, low),
@@ -350,10 +379,12 @@
             pltpu.VMEM((mine, 4 * rows, d), low),
             pltpu.VMEM((mine, 4 * rows, d), low),
             pltpu.VMEM((2, 3 * rows, rows), full),
-            pltpu.VMEM((3 * rows, group * rows), low),
-            pltpu.VMEM((3 * rows, group * rows), low),
-            pltpu.VMEM((4 * rows, d), full),
-            pltpu.VMEM((4 * rows, d), full),
+            pltpu.VMEM((mine, 2, 3 * rows, group * rows), low),
+            pltpu.VMEM((mine, 2, 3 * rows, group * rows), low),
+            pltpu.VMEM((rows, d), full),
+            pltpu.VMEM((rows, d), full),
+            pltpu.VMEM((2, rows, d), full),
+            pltpu.VMEM((2, rows, d), full),
             pltpu.VMEM((mine, rows, d), full),
             pltpu.VMEM((mine, rows, d), full),
             pltpu.VMEM((mine, 3, rows, d), low),
@@ -375,6 +406,14 @@
         compiler_params=pltpu.CompilerParams(collective_id=0, has_side_effects=True),
         name="packed_attention_backward",
     )(doc_lengths, queries, keys, values, attn_out, output_gradient)
+    return pl.pallas_call(
+        store_kernel,
+        out_shape=tuple(jax.ShapeDtypeStruct(r.shape, low) for r in results),
+        in_specs=[pl.BlockSpec(memory_space=pltpu.VMEM)] * 3,
+        out_specs=(any_space,) * 3,
+        scratch_shapes=[dma((3,))],
+        name="store_gradients",
+    )(*[pltpu.with_memory_space_constraint(r, pltpu.VMEM) for r in results])
 
 
 def solution(mesh):

time: 23.6 us -> 20.9 us (0.89)
  the two profiles are of different devices: /device:TPU:23 before, /device:TPU:17 now
where the time goes in v3:
time: 20.9 us; the launch traced here: 20.7 us
  Pallas kernels  20.1 us (96%)
  between operations  0.64 us (3%)
    pallas_call x1, Pallas kernels, on_device(): pl.pallas_call(functools.partial(kernel, n_ctx, group, mine), out_shape=(...  19 us
    pallas_call x1, Pallas kernels, on_device(): pl.pallas_call(store_kernel, out_shape=tuple((jax.ShapeDtypeStruct(r.shap...  1.07 us

profile of v3, /device:TPU:17, one launch (start us, length us, event | category | flops | bytes accessed | tf_op | source)
XLA Modules:
  0.0 20.7 jit_solution(11588117772118118838)
XLA Ops:
  0.6 19.0 %packed_attention_backward.1 = (bf16[128,4096]{1,0:T(8,128)(2,1)S(1)}, bf16[128,512]{1,0:T(8,128)(2,1)S(1)}, bf16[128,512]{1,0:T(8,128)(2,1)S(1)}) custom-call(s32[32]{0:T(128)} %doc_ref.1, bf16[128,4096]{1,0:T(8,128)(2,1)} %q_hbm.1, bf16[128,512]{1,0:T(8,128)(2,1)} %k_hbm.1, bf16[128,512]{1,0:T(8,128)(2,1)} %v_hbm.1, bf16[128,4096]{1,0:T(8,128)(2,1)} %o_hbm.1, ...), custom_call_target="tpu_custom_call" | custom-call | tf_op jit(solution)/shard_map/packed_attention_backward/pallas_call | solution.py:363
  19.7 1.1 %store_gradients.1 = (bf16[128,4096]{1,0:T(8,128)(2,1)}, bf16[128,512]{1,0:T(8,128)(2,1)}, bf16[128,512]{1,0:T(8,128)(2,1)}) custom-call(bf16[128,4096]{1,0:T(8,128)(2,1)S(1)} %get-tuple-element.6.dq, bf16[128,512]{1,0:T(8,128)(2,1)S(1)} %get-tuple-element.7.dk, bf16[128,512]{1,0:T(8,128)(2,1)S(1)} %get-tuple-element.8.dv), custom_call_target="tpu_custom_call" | custom-call | tf_op jit(solution)/shard_map/store_gradients/pallas_call | solution.py:409

commit v4 on v3

--- a/solution.py
+++ b/solution.py
@@ -301,17 +301,19 @@
             query_part(i, token_block)
 
     for i in range(mine_count):
+        dq_out[:, block(me * mine_count + i, wide)] = dq_buf[i, me]
+    for i in range(mine_count):
         for copy in across(i, other)[5:]:
             copy.wait_recv()
-
+        dq_out[:, block(other * mine_count + i, wide)] = dq_got[i]
+
+    for i in range(mine_count):
         @pl.when(has_next)
         def _():
             for source in range(2):
                 for copy in give_back(i, source, me):
                     copy.wait_recv()
 
-        dq_out[:, block(other * mine_count + i, wide)] = dq_got[i]
-        dq_out[:, block(me * mine_count + i, wide)] = dq_buf[i, me]
         for own, part, late, out in (
             (own_k, part_k, next_k, dk_out), (own_v, part_v, next_v, dv_out)
         ):

time: 20.9 us -> 20.9 us (level)
  no operation moved by 1% of the time
where the time goes in v4:
time: 20.9 us; the launch traced here: 20.7 us
  Pallas kernels  20.1 us (96%)
  between operations  0.64 us (3%)
    pallas_call x1, Pallas kernels, on_device(): pl.pallas_call(functools.partial(kernel, n_ctx, group, mine), out_shape=(...  19 us
    pallas_call x1, Pallas kernels, on_device(): pl.pallas_call(store_kernel, out_shape=tuple((jax.ShapeDtypeStruct(r.shap...  1.07 us

profile of v4, /device:TPU:17, one launch (start us, length us, event | category | flops | bytes accessed | tf_op | source)
XLA Modules:
  0.0 20.7 jit_solution(15182987306807604039)
XLA Ops:
  0.6 19.0 %packed_attention_backward.1 = (bf16[128,4096]{1,0:T(8,128)(2,1)S(1)}, bf16[128,512]{1,0:T(8,128)(2,1)S(1)}, bf16[128,512]{1,0:T(8,128)(2,1)S(1)}) custom-call(s32[32]{0:T(128)} %doc_ref.1, bf16[128,4096]{1,0:T(8,128)(2,1)} %q_hbm.1, bf16[128,512]{1,0:T(8,128)(2,1)} %k_hbm.1, bf16[128,512]{1,0:T(8,128)(2,1)} %v_hbm.1, bf16[128,4096]{1,0:T(8,128)(2,1)} %o_hbm.1, ...), custom_call_target="tpu_custom_call" | custom-call | tf_op jit(solution)/shard_map/packed_attention_backward/pallas_call | solution.py:365
  19.7 1.1 %store_gradients.1 = (bf16[128,4096]{1,0:T(8,128)(2,1)}, bf16[128,512]{1,0:T(8,128)(2,1)}, bf16[128,512]{1,0:T(8,128)(2,1)}) custom-call(bf16[128,4096]{1,0:T(8,128)(2,1)S(1)} %get-tuple-element.6.dq, bf16[128,512]{1,0:T(8,128)(2,1)S(1)} %get-tuple-element.7.dk, bf16[128,512]{1,0:T(8,128)(2,1)S(1)} %get-tuple-element.8.dv), custom_call_target="tpu_custom_call" | custom-call | tf_op jit(solution)/shard_map/store_gradients/pallas_call | solution.py:411
